TPU v7x, 256 devices: a whole 4x4x8 slice. The times are simulated.
256 devices in a mesh: leaf: 32 (over x, y, core), col: 8 (over z).
Axes of the slice: x: 4, y: 4, z: 8, core: 2. Of those that a mesh axis runs over, the one named last changes fastest.
Arguments:
- near: float32 [512, 13, 256, 256], P(('leaf', 'col')), may hold values from -1 to 6, as said below
- basis: float32 [512, 256, 256], P(('leaf', 'col')), may hold values from -1 to 2
- parent_basis: float32 [128, 256, 256], P('leaf'), may hold values from -1 to 2
- grand_basis: float32 [32, 256, 256], P('leaf'), may hold values from -1 to 2
- nbr: int32 [512, 13], P(('leaf', 'col')), may hold values from 0 to 511, as said below
- live: int32 [512, 13], P(('leaf', 'col')), may hold values from 0 to 1, as said below
- partner: int32 [512, 13], P(('leaf', 'col')), may hold values from 0 to 12, as said below
Outputs:
- leaf_schur: float32 [512, 64, 832], P(('leaf', 'col'))
- parent_schur: float32 [128, 64, 256], P('leaf')
- top_schur: float32 [32, 64, 64], P('leaf')
Inputs may be any that keep to these rules, and one draw needn't show every extreme that they name: nbr[j,0] is j; the other 12 slots name distinct leaves at distances 1 to 6 from j in leaf order, taken around the cycle of 512 leaves, in an order drawn per leaf. Slot 0 and the slots of leaves of the same group of four are always 1; live at (nbr[j,k], partner[j,k]) equals live[j,k]; some leaf has all 13 slots 1. nbr[nbr[j,k], partner[j,k]] is j; partner[j,0] is 0. near holds blocks of one symmetric matrix: the block at (nbr[j,k], partner[j,k]) is the transpose of near[j,k], and near[j,0] is symmetric positive definite.
All inputs are finite; a program needn't handle non-finite values.
Results may differ from a plain program's by a relative error of at most 0.000078.
Values sent between devices are 32-bit elements; how exact they have to be, the bound alone decides.
A program may use at most 128 MiB of HBM per device.

v0:
```python
import jax
import jax.numpy as jnp
from jax import lax
from jax.sharding import PartitionSpec as P

M = 256
SK = 64
RD = 192
NB = 13
REACH = 6


FULL_PRECISION = lax.Precision.HIGHEST


def shifted(value, axis, steps):
    count = lax.axis_size(axis)
    pairs = [(source, (source + steps) % count) for source in range(count)]
    return lax.ppermute(value, axis, pairs)


def eliminate(diag_block, columns):
    redundant = diag_block.shape[-1] - SK
    factor = jnp.linalg.cholesky(diag_block[:, :redundant, :redundant])
    solved = jax.scipy.linalg.cho_solve((factor, True), diag_block[:, :redundant, redundant:])
    coupled = jnp.einsum(
        "nrs,nrw->nsw", solved, columns[:, :redundant, :], precision=FULL_PRECISION
    )
    return (coupled, columns[:, redundant:, :] - coupled)


def parent_level(stacked, own_basis, family, position):
    parents = stacked.shape[0]
    turned = jnp.einsum("nab,nac->nbc", own_basis, stacked, precision=FULL_PRECISION).reshape(
        parents, M, 4, M
    )
    chooser = jax.nn.one_hot(position, 4, dtype=jnp.float32)
    own_cols = jnp.einsum("nbqc,nq->nbc", turned, chooser, precision=FULL_PRECISION)
    diag_block = jnp.einsum("nbc,ncd->nbd", own_cols, own_basis, precision=FULL_PRECISION)
    columns = jnp.einsum("nbqc,nqcd->nbqd", turned, family, precision=FULL_PRECISION).reshape(
        parents, M, 4 * SK
    )
    return eliminate(diag_block, columns)


def mirror_rows(coupled, remainder):
    grand_count = coupled.shape[0] // 4
    blocks = coupled.reshape(grand_count, 4, SK, 4, SK)
    mirrored = jnp.einsum("gqypx->gpxqy", blocks)
    apart = 1.0 - jnp.eye(4, dtype=jnp.float32)
    result = remainder.reshape(grand_count, 4, SK, 4, SK) - mirrored * apart[None, :, None, :, None]
    return result.reshape(grand_count * 4, SK, 4 * SK)


def top_level(parent_schur, grand_basis):
    joined = parent_schur.reshape(-1, M, M)
    turned = jnp.einsum("gab,gac->gbc", grand_basis, joined, precision=FULL_PRECISION)
    grand_block = jnp.einsum("gbc,gcd->gbd", turned, grand_basis, precision=FULL_PRECISION)
    coupled, remainder = eliminate(grand_block, grand_block[:, :, RD:])
    return remainder


def panel_window(panels, hop_count):
    below_list = []
    above_list = []
    for hop_index in range(1, hop_count + 1):
        below_list.append(shifted(panels, ("leaf", "col"), hop_index))
        above_list.append(shifted(panels, ("leaf", "col"), -hop_index))
    return jnp.concatenate(below_list[::-1] + [panels] + above_list, axis=0)


def reply_window(replies, hop_count):
    below_list = []
    above_list = []
    for hop_index in range(1, hop_count + 1):
        below_list.append(shifted(replies, ("leaf", "col"), hop_index))
        above_list.append(shifted(replies, ("leaf", "col"), -hop_index))
    return jnp.concatenate(below_list[::-1] + [replies] + above_list, axis=0)


def pick_slots(window, slot_spots):
    flattened = window.reshape((-1,) + window.shape[2:])
    chosen = jnp.take(flattened, slot_spots.reshape(-1), axis=0)
    return chosen.reshape(slot_spots.shape + window.shape[2:])


def on_device(near, basis, parent_basis, grand_basis, nbr, live, partner):
    leaf_count = near.shape[0]
    device_total = lax.axis_size(("leaf", "col"))
    leaf_total = leaf_count * device_total
    first_leaf = lax.axis_index(("leaf", "col")) * leaf_count
    hop_count = (REACH + leaf_count - 1) // leaf_count
    local_ids = first_leaf + jnp.arange(leaf_count, dtype=jnp.int32)
    offset = (nbr - local_ids[:, None] + leaf_total // 2) % leaf_total - leaf_total // 2
    leaf_spots = hop_count * leaf_count + jnp.arange(leaf_count, dtype=jnp.int32)[:, None] + offset
    slot_spots = leaf_spots * NB + partner
    weights = live.astype(jnp.float32)
    panels = (
        jnp.einsum("jkab,jbc->jkca", near, basis[:, :, RD:], precision=FULL_PRECISION)
        * weights[:, :, None, None]
    )
    fetched = pick_slots(panel_window(panels, hop_count), slot_spots)
    rotated = jnp.einsum("iqca,iab->ibqc", fetched, basis, precision=FULL_PRECISION).reshape(
        leaf_count, M, NB * SK
    )
    rows_first = jnp.einsum("iab,iac->ibc", basis, near[:, 0], precision=FULL_PRECISION)
    diag_block = jnp.einsum("ibc,icd->ibd", rows_first, basis, precision=FULL_PRECISION)
    coupled, remainder = eliminate(diag_block, rotated)
    replies = (
        coupled.reshape(leaf_count, SK, NB, SK)
        .transpose(0, 2, 1, 3)
        .reshape(leaf_count, NB, SK * SK)
    )
    returned = pick_slots(reply_window(replies, hop_count), slot_spots).reshape(
        leaf_count, NB, SK, SK
    )
    others = (jnp.arange(NB) > 0).astype(jnp.float32)
    leaf_schur = remainder.reshape(leaf_count, SK, NB, SK) - jnp.einsum(
        "iqba,q->iaqb", returned, others
    )
    targets = (local_ids // 16 * 16)[:, None, None] + jnp.arange(16, dtype=jnp.int32)[None, None, :]
    member = (nbr[:, :, None] == targets).astype(jnp.float32)
    grand_rows = jnp.einsum("iaqb,iqw->iawb", leaf_schur, member, precision=FULL_PRECISION).reshape(
        leaf_count, SK, 16 * SK
    )
    skel_all = parent_basis[:, :, RD:].reshape(-1, 4, M, SK)
    all_rows = lax.all_gather(grand_rows, "col", axis=0, tiled=True)
    parents_here = parent_basis.shape[0]
    stacked = all_rows.reshape(parents_here, M, 4 * M)
    family = jnp.repeat(skel_all, 4, axis=0)
    position = jnp.arange(parents_here, dtype=jnp.int32) % 4
    coupled_up, remainder_up = parent_level(stacked, parent_basis, family, position)
    parent_schur = mirror_rows(coupled_up, remainder_up)
    return (
        leaf_schur.reshape(leaf_count, SK, NB * SK),
        parent_schur,
        top_level(parent_schur, grand_basis),
    )


def solution(mesh):
    return jax.shard_map(
        on_device,
        mesh=mesh,
        in_specs=(
            P(("leaf", "col"), None, None, None),
            P(("leaf", "col"), None, None),
            P("leaf", None, None),
            P("leaf", None, None),
            P(("leaf", "col"), None),
            P(("leaf", "col"), None),
            P(("leaf", "col"), None),
        ),
        out_specs=(P(("leaf", "col"), None, None), P("leaf", None, None), P("leaf", None, None)),
        check_vma=False,
    )
```

profile of v0, /device:TPU:32, one launch (start us, length us, event | category | flops | bytes accessed | tf_op | source)
XLA Modules:
  0.0 721.3 jit_solution(13428649760985542080)
XLA Ops:
  7.9 9.2 %multiply_bitcast_fusion = f32[2,13,64,256]{3,2,1,0:T(8,128)S(1)} fusion(f32[2,13,256,256]{3,2,1,0:T(8,128)} %param.7, f32[2,13]{1,0:T(2,128)S(1)} %convert_element_type.14, f32[2,256,256]{2,1,0:T(8,128)} %param.8), kind=kOutput, calls=%fused_computation.6 | convolution fusion | flops 1309048832 | bytes 8781928 | tf_op jit(solution)/shard_map/jkab,jbc->jkca/dot_general | solution.py:99
  17.2 5.9 collective-permute-start
  23.1 1.5 collective-permute-start.1
  26.6 6.0 collective-permute-start.4
  32.6 2.1 fusion.14
  41.0 23.6 %custom-call.60 = f32[2,128,128]{2,1,0:T(8,128)S(1)} custom-call(f32[2,128,128]{2,1,0:T(8,128)S(1)} %cholesky.372), custom_call_target="Cholesky" | custom-call | tf_op jit(solution)/shard_map/jit(cholesky)/cholesky | solution.py:24
  64.7 2.0 select_reduce_fusion.2
  66.7 20.5 %custom-call.61 = f32[2,1,128,128]{2,3,1,0:T(8,128)S(1)} custom-call(f32[2,1,128,128]{3,2,1,0:T(8,128)} %get-tuple-element.82), custom_call_target="InvertDiagBlocksLowerTriangular" | custom-call | tf_op jit(solution)/shard_map/jit(cholesky)/cholesky | solution.py:24
  87.1 1.1 constant_dynamic-update-slice_fusion.11
  88.2 1.1 convolution_subtract_fusion.5
  89.3 11.7 %custom-call.62 = f32[2,64,64]{2,1,0:T(8,128)S(1)} custom-call(f32[2,64,64]{2,1,0:T(8,128)S(1)} %convolution_subtract_fusion.5), custom_call_target="Cholesky" | custom-call | tf_op jit(solution)/shard_map/jit(cholesky)/cholesky | solution.py:24
  105.3 40.1 %custom-call.63 = f32[2,2,128,128]{2,3,1,0:T(8,128)S(1)} custom-call(f32[2,2,128,128]{3,2,1,0:T(8,128)} %pad_maximum_fusion.1), custom_call_target="InvertDiagBlocksLowerTriangular" | custom-call | tf_op jit(solution)/shard_map/jit(_cho_solve)/vmap()/triangular_solve | solution.py:25
  145.6 1.1 convolution_subtract_fusion.4
  149.8 1.6 constant_dynamic-update-slice_fusion.6
  151.4 59.0 %collective-permute-done.1 = f32[2,13,64,256]{3,2,1,0:T(8,128)} collective-permute-done((f32[2,13,64,256]{3,2,1,0:T(8,128)S(1)}, f32[2,13,64,256]{3,2,1,0:T(8,128)}, u32[]{:S(2)}, u32[]{:S(2)}) %collective-permute-start.1) | collective-permute-done | bytes 1703968 | tf_op jit(solution)/shard_map/ppermute | solution.py:19
  210.4 1.6 constant_dynamic-update-slice_fusion.5
  212.0 29.8 %collective-permute-done.2 = f32[2,13,64,256]{3,2,1,0:T(8,128)} collective-permute-done((f32[2,13,64,256]{3,2,1,0:T(8,128)S(1)}, f32[2,13,64,256]{3,2,1,0:T(8,128)}, u32[]{:S(2)}, u32[]{:S(2)}) %collective-permute-start.2) | collective-permute-done | bytes 1703968 | tf_op jit(solution)/shard_map/ppermute | solution.py:19
  241.8 1.6 constant_dynamic-update-slice_fusion.4
  243.5 1.6 constant_dynamic-update-slice_fusion.2
  245.1 1.6 constant_dynamic-update-slice_fusion.1
  246.7 12.3 %collective-permute-done.5 = f32[2,13,64,256]{3,2,1,0:T(8,128)S(1)} collective-permute-done((f32[2,13,64,256]{3,2,1,0:T(8,128)S(1)}, f32[2,13,64,256]{3,2,1,0:T(8,128)S(1)}, u32[]{:S(2)}, u32[]{:S(2)}) %collective-permute-start.5) | collective-permute-done | bytes 1703968 | tf_op jit(solution)/shard_map/ppermute | solution.py:19
  259.2 4.4 copy-done.6
  263.6 6.3 gather_fusion
  269.9 3.1 fusion.2
  273.6 2.4 fusion.87
  276.0 1.3 reshape.376
  278.1 1.3 collective-permute-start.7
  279.4 1.5 collective-permute-start.8
  281.5 6.3 collective-permute-start.10
  287.7 22.6 %collective-permute-done.6 = f32[2,13,4096]{2,0,1:T(2,128)S(1)} collective-permute-done((f32[2,13,4096]{2,0,1:T(2,128)S(1)}, f32[2,13,4096]{2,0,1:T(2,128)S(1)}, u32[]{:S(2)}, u32[]{:S(2)}) %collective-permute-start.6) | collective-permute-done | bytes 426016 | tf_op jit(solution)/shard_map/ppermute | solution.py:19
  311.4 1.3 reshape.375
  312.7 18.1 %collective-permute-done.7 = f32[2,13,4096]{2,0,1:T(2,128)S(1)} collective-permute-done((f32[2,13,4096]{2,0,1:T(2,128)S(1)}, f32[2,13,4096]{2,0,1:T(2,128)S(1)}, u32[]{:S(2)}, u32[]{:S(2)}) %collective-permute-start.7) | collective-permute-done | bytes 426016 | tf_op jit(solution)/shard_map/ppermute | solution.py:19
  330.8 3.8 collective-permute-done.8
  334.7 8.7 %concatenate.61 = f32[14,13,4096]{2,0,1:T(8,128)} concatenate(f32[2,13,4096]{2,0,1:T(2,128)S(1)} %collective-permute-done.6, f32[2,13,4096]{2,0,1:T(2,128)S(1)} %collective-permute-done.7, f32[2,13,4096]{2,0,1:T(2,128)S(1)} %collective-permute-done.8, f32[2,13,4096]{2,0,1:T(2,128)S(1)} %reshape.377, f32[2,13,4096]{2,0,1:T(2,128)S(1)} %collective-permute-done.9, ...), dimensions={0} | concatenate | bytes 5963776 | tf_op jit(solution)/shard_map/concatenate | solution.py:78
  343.4 5.5 copy.123
  348.9 2.2 reshape.378
  351.2 1.5 gather_fusion.1
  352.7 1.4 gather.33
  354.6 1.4 bitcast_subtract_fusion
  356.6 1.1 reshape.380
  358.9 1.1 reshape.379
  359.9 58.7 %all-gather.2.cloned.1.call-done = f32[16,64,1024]{2,1,0:T(8,128)} async-done(((f32[2,64,1024]{2,1,0:T(8,128)}), f32[16,64,1024]{2,1,0:T(8,128)}) %all-gather.2.cloned.1.call-update) | async-done | bytes 4194320 | tf_op jit(solution)/shard_map/all_gather | solution.py:127
  418.6 10.8 %fusion.90 = f32[4,1024,256]{2,1,0:T(8,128)} fusion(f32[4,256,1024]{2,1,0:T(8,128)} %bitcast.209, f32[4,256,256]{2,1,0:T(8,128)S(1)} %copy-done.1), kind=kOutput, calls=%fused_computation.191 | convolution fusion | flops 3221225472 | bytes 9437184 | tf_op jit(solution)/shard_map/nab,nac->nbc/dot_general | solution.py:34
  429.4 5.4 copy.162
  434.8 6.5 fusion.72
  441.3 1.9 fusion.8
  444.6 46.9 %custom-call.64 = f32[4,128,128]{2,1,0:T(8,128)S(1)} custom-call(f32[4,128,128]{2,1,0:T(8,128)S(1)} %cholesky.375), custom_call_target="Cholesky" | custom-call | tf_op jit(solution)/shard_map/jit(cholesky)/cholesky | solution.py:24
  491.6 39.5 %custom-call.65 = f32[4,1,128,128]{2,3,1,0:T(8,128)S(1)} custom-call(f32[4,1,128,128]{3,2,1,0:T(8,128)S(1)} %get-tuple-element.78), custom_call_target="InvertDiagBlocksLowerTriangular" | custom-call | tf_op jit(solution)/shard_map/jit(cholesky)/cholesky | solution.py:24
  531.2 1.3 constant_dynamic-update-slice_fusion.9
  532.5 1.2 convolution_subtract_fusion.2
  533.7 23.5 %custom-call.66 = f32[4,64,64]{2,1,0:T(8,128)S(1)} custom-call(f32[4,64,64]{2,1,0:T(8,128)S(1)} %convolution_subtract_fusion.2), custom_call_target="Cholesky" | custom-call | tf_op jit(solution)/shard_map/jit(cholesky)/cholesky | solution.py:24
  559.0 5.0 fusion.18
  565.0 1.9 copy.182
  568.0 1.8 pad_maximum_fusion
  569.8 80.3 %custom-call.67 = f32[4,2,128,128]{2,3,1,0:T(8,128)} custom-call(f32[4,2,128,128]{3,2,1,0:T(8,128)} %pad_maximum_fusion), custom_call_target="InvertDiagBlocksLowerTriangular" | custom-call | tf_op jit(solution)/shard_map/jit(_cho_solve)/vmap()/triangular_solve | solution.py:25
  650.1 1.3 fusion.34
  651.7 1.2 fusion.47
  652.9 1.2 fusion.46
  654.4 1.6 fusion.33
  656.0 2.0 fusion.88
  660.3 11.7 %custom-call.68 = f32[1,128,128]{2,1,0:T(8,128)S(1)} custom-call(f32[1,128,128]{2,1,0:T(8,128)S(1)} %cholesky.378), custom_call_target="Cholesky" | custom-call | tf_op jit(solution)/shard_map/jit(cholesky)/cholesky | solution.py:24
  672.0 9.8 %custom-call.69 = f32[1,1,128,128]{2,3,1,0:T(8,128)S(1)} custom-call(f32[1,1,128,128]{3,2,1,0:T(8,128)S(1)} %get-tuple-element.84), custom_call_target="InvertDiagBlocksLowerTriangular" | custom-call | tf_op jit(solution)/shard_map/jit(cholesky)/cholesky | solution.py:24
  682.2 5.8 custom-call.70
  691.7 20.0 %custom-call.71 = f32[2,128,128]{1,2,0:T(8,128)S(1)} custom-call(f32[2,128,128]{2,1,0:T(8,128)S(1)} %pad_maximum_fusion.2), custom_call_target="InvertDiagBlocksLowerTriangular" | custom-call | tf_op jit(solution)/shard_map/jit(_cho_solve)/triangular_solve | solution.py:25
  (134 shorter events, 35.1 us)
Async XLA Ops:
  7.2 651.9 %copy-start = (f32[1,256,256]{2,1,0:T(8,128)S(1)}, f32[1,256,256]{2,1,0:T(8,128)}, u32[]{:S(2)}) copy-start(f32[1,256,256]{2,1,0:T(8,128)} %param.10) | copy-start | bytes 786436
  7.2 411.4 %all-gather.2.cloned.1.call-start = ((), (), s32[]{:S(2)}) async-start(), calls=%async_computation | async-start | bytes 4718592 | tf_op jit(solution)/shard_map/all_gather | solution.py:127
  7.9 24.7 %copy-start.2 = (f32[2,256,256]{2,1,0:T(8,128)S(1)}, f32[2,256,256]{2,1,0:T(8,128)}, u32[]{:S(2)}) copy-start(f32[2,256,256]{2,1,0:T(8,128)} %param.8) | copy-start | bytes 1572868
  17.2 130.7 %collective-permute-start = (f32[2,13,64,256]{3,2,1,0:T(8,128)S(1)}, f32[2,13,64,256]{3,2,1,0:T(8,128)}, u32[]{:S(2)}, u32[]{:S(2)}) collective-permute-start(f32[2,13,64,256]{3,2,1,0:T(8,128)S(1)} %multiply_bitcast_fusion), channel_id=1, source_target_pairs={{0,3},{1,4},{2,5},{3,6},{4,7},{5,8},{6,9},{7,10},{8,11},{9,12},{10... | collective-permute-start | bytes 5111816 | tf_op jit(solution)/shard_map/ppermute | solution.py:19
  23.1 187.3 %collective-permute-start.1 = (f32[2,13,64,256]{3,2,1,0:T(8,128)S(1)}, f32[2,13,64,256]{3,2,1,0:T(8,128)}, u32[]{:S(2)}, u32[]{:S(2)}) collective-permute-start(f32[2,13,64,256]{3,2,1,0:T(8,128)S(1)} %multiply_bitcast_fusion), channel_id=1, source_target_pairs={{0,2},{1,3},{2,4},{3,5},{4,6},{5,7},{6,8},{7,9},{8,10},{9,11},{10,... | collective-permute-start | bytes 5111816 | tf_op jit(solution)/shard_map/ppermute | solution.py:19
  24.6 217.2 %collective-permute-start.2 = (f32[2,13,64,256]{3,2,1,0:T(8,128)S(1)}, f32[2,13,64,256]{3,2,1,0:T(8,128)}, u32[]{:S(2)}, u32[]{:S(2)}) collective-permute-start(f32[2,13,64,256]{3,2,1,0:T(8,128)S(1)} %multiply_bitcast_fusion), channel_id=1, source_target_pairs={{0,1},{1,2},{2,3},{3,4},{4,5},{5,6},{6,7},{7,8},{8,9},{9,10},{10,1... | collective-permute-start | bytes 5111816 | tf_op jit(solution)/shard_map/ppermute | solution.py:19
  25.6 217.9 %collective-permute-start.3 = (f32[2,13,64,256]{3,2,1,0:T(8,128)S(1)}, f32[2,13,64,256]{3,2,1,0:T(8,128)}, u32[]{:S(2)}, u32[]{:S(2)}) collective-permute-start(f32[2,13,64,256]{3,2,1,0:T(8,128)S(1)} %multiply_bitcast_fusion), channel_id=1, source_target_pairs={{0,255},{1,0},{2,1},{3,2},{4,3},{5,4},{6,5},{7,6},{8,7},{9,8},{10,... | collective-permute-start | bytes 5111816 | tf_op jit(solution)/shard_map/ppermute | solution.py:19
  26.6 218.5 %collective-permute-start.4 = (f32[2,13,64,256]{3,2,1,0:T(8,128)S(1)}, f32[2,13,64,256]{3,2,1,0:T(8,128)}, u32[]{:S(2)}, u32[]{:S(2)}) collective-permute-start(f32[2,13,64,256]{3,2,1,0:T(8,128)S(1)} %multiply_bitcast_fusion), channel_id=1, source_target_pairs={{0,254},{1,255},{2,0},{3,1},{4,2},{5,3},{6,4},{7,5},{8,6},{9,7},{1... | collective-permute-start | bytes 5111816 | tf_op jit(solution)/shard_map/ppermute | solution.py:19
  40.3 0.7 copy-start.5
  103.6 0.9 copy-start.4
  147.9 111.1 %collective-permute-start.5 = (f32[2,13,64,256]{3,2,1,0:T(8,128)S(1)}, f32[2,13,64,256]{3,2,1,0:T(8,128)S(1)}, u32[]{:S(2)}, u32[]{:S(2)}) collective-permute-start(f32[2,13,64,256]{3,2,1,0:T(8,128)S(1)} %multiply_bitcast_fusion), channel_id=1, source_target_pairs={{0,253},{1,254},{2,255},{3,0},{4,1},{5,2},{6,3},{7,4},{8,5},{9,6},... | collective-permute-start | bytes 5111816 | tf_op jit(solution)/shard_map/ppermute | solution.py:19
  259.2 4.4 copy-start.6
  278.0 32.3 %collective-permute-start.6 = (f32[2,13,4096]{2,0,1:T(2,128)S(1)}, f32[2,13,4096]{2,0,1:T(2,128)S(1)}, u32[]{:S(2)}, u32[]{:S(2)}) collective-permute-start(f32[2,13,4096]{2,0,1:T(2,128)S(1)} %reshape.377), channel_id=1, source_target_pairs={{0,3},{1,4},{2,5},{3,6},{4,7},{5,8},{6,9},{7,10},{8,11},{9,12},{10... | collective-permute-start | bytes 1277960 | tf_op jit(solution)/shard_map/ppermute | solution.py:19
  278.1 52.7 %collective-permute-start.7 = (f32[2,13,4096]{2,0,1:T(2,128)S(1)}, f32[2,13,4096]{2,0,1:T(2,128)S(1)}, u32[]{:S(2)}, u32[]{:S(2)}) collective-permute-start(f32[2,13,4096]{2,0,1:T(2,128)S(1)} %reshape.377), channel_id=1, source_target_pairs={{0,2},{1,3},{2,4},{3,5},{4,6},{5,7},{6,8},{7,9},{8,10},{9,11},{10,... | collective-permute-start | bytes 1277960 | tf_op jit(solution)/shard_map/ppermute | solution.py:19
  279.4 55.2 %collective-permute-start.8 = (f32[2,13,4096]{2,0,1:T(2,128)S(1)}, f32[2,13,4096]{2,0,1:T(2,128)S(1)}, u32[]{:S(2)}, u32[]{:S(2)}) collective-permute-start(f32[2,13,4096]{2,0,1:T(2,128)S(1)} %reshape.377), channel_id=1, source_target_pairs={{0,1},{1,2},{2,3},{3,4},{4,5},{5,6},{6,7},{7,8},{8,9},{9,10},{10,1... | collective-permute-start | bytes 1277960 | tf_op jit(solution)/shard_map/ppermute | solution.py:19
  280.9 53.7 %collective-permute-start.9 = (f32[2,13,4096]{2,0,1:T(2,128)S(1)}, f32[2,13,4096]{2,0,1:T(2,128)S(1)}, u32[]{:S(2)}, u32[]{:S(2)}) collective-permute-start(f32[2,13,4096]{2,0,1:T(2,128)S(1)} %reshape.377), channel_id=1, source_target_pairs={{0,255},{1,0},{2,1},{3,2},{4,3},{5,4},{6,5},{7,6},{8,7},{9,8},{10,... | collective-permute-start | bytes 1277960 | tf_op jit(solution)/shard_map/ppermute | solution.py:19
  281.5 53.1 %collective-permute-start.10 = (f32[2,13,4096]{2,0,1:T(2,128)S(1)}, f32[2,13,4096]{2,0,1:T(2,128)}, u32[]{:S(2)}, u32[]{:S(2)}) collective-permute-start(f32[2,13,4096]{2,0,1:T(2,128)S(1)} %reshape.377), channel_id=1, source_target_pairs={{0,254},{1,255},{2,0},{3,1},{4,2},{5,3},{6,4},{7,5},{8,6},{9,7},{1... | collective-permute-start | bytes 1277960 | tf_op jit(solution)/shard_map/ppermute | solution.py:19
  310.3 24.4 %collective-permute-start.11 = (f32[2,13,4096]{2,0,1:T(2,128)S(1)}, f32[2,13,4096]{2,0,1:T(2,128)}, u32[]{:S(2)}, u32[]{:S(2)}) collective-permute-start(f32[2,13,4096]{2,0,1:T(2,128)S(1)} %reshape.377), channel_id=1, source_target_pairs={{0,253},{1,254},{2,255},{3,0},{4,1},{5,2},{6,3},{7,4},{8,5},{9,6},... | collective-permute-start | bytes 1277960 | tf_op jit(solution)/shard_map/ppermute | solution.py:19
  352.6 3.4 copy-start.11
  354.0 3.7 copy-start.1
  443.2 48.4 %copy-start.8 = (pred[128,128]{1,0:T(8,128)(4,1)S(1)}, pred[128,128]{1,0:T(8,128)(4,1)}, u32[]{:S(2)}) copy-start(pred[128,128]{1,0:T(8,128)(4,1)} %get-tuple-element.102) | copy-start | bytes 49156
  443.2 114.1 %copy-start.9 = (pred[64,64]{1,0:T(8,128)(4,1)S(1)}, pred[64,64]{1,0:T(8,128)(4,1)}, u32[]{:S(2)}) copy-start(pred[64,64]{1,0:T(8,128)(4,1)} %iota_compare_fusion.11) | copy-start | bytes 12292
  443.2 114.2 %copy-start.7 = (pred[192,192]{1,0:T(8,128)(4,1)S(1)}, pred[192,192]{1,0:T(8,128)(4,1)}, u32[]{:S(2)}) copy-start(pred[192,192]{1,0:T(8,128)(4,1)} %iota_compare_fusion.2) | copy-start | bytes 110596
  443.7 0.9 copy-start.3
  566.9 91.6 %copy-start.10 = (f32[4,4]{0,1:T(4,128)S(1)}, f32[4,4]{0,1:T(4,128)}, u32[]{:S(2)}) copy-start(f32[4,4]{0,1:T(4,128)} %convert_subtract_fusion) | copy-start | bytes 196
Sparse Core Ops, SparseCore 0:
  357.9 60.6 all-gather.1
where the time goes:
time: 735 us; the launch traced here: 721 us
  other arithmetic  352 us (48%)
  waiting for transfers between devices  204 us (28%)
  matrix products  61.2 us (8%)
  local copies, waits for them, and re-layouts  60.5 us (8%)
  starting transfers between devices  26.6 us (4%)
  between operations  16.7 us (2%)
    another operation x25, other arithmetic, eliminate(): factor = jnp.linalg.cholesky(diag_block[:, :redundant, :redundant])  200 us
    another operation x15, other arithmetic, eliminate(): jax.scipy.linalg.cho_solve((factor, True), diag_block[:, :redundant, redu...  147 us
    ppermute x12, waiting for transfers between devices, shifted(): return lax.ppermute(value, axis, pairs)  146 us
    all_gather x1, waiting for transfers between devices, on_device(): all_rows = lax.all_gather(grand_rows, 'col', axis=0, tiled=True)  58.7 us
    ppermute x12, starting transfers between devices, shifted(): return lax.ppermute(value, axis, pairs)  26.5 us
    unnamed x33, local copies, waits for them, and re-layouts  16.9 us
  transfers between devices with their start and end apart: 13, of which 8 were waited for; matrix products, arithmetic and copies ran while one was open for 18% of the time, Pallas kernels for 0%

commit v1 on v0

v1 whole, which is shorter than its diff:
```python
import functools

import jax
import jax.numpy as jnp
from jax import lax
from jax.experimental import pallas as pl
from jax.experimental.pallas import tpu as pltpu
from jax.sharding import PartitionSpec as P

M = 256
SK = 64
RD = 192
NB = 13
G = 16
F32 = jnp.float32
HIGH = lax.Precision.HIGH
MESH = pl.DeviceIdType.MESH
NN = ((1,), (0,))
NT = ((1,), (1,))
TN = ((0,), (0,))


def mm(a, b, dims=NN):
    return lax.dot_general(a, b, (dims, ((), ())), precision=HIGH, preferred_element_type=F32)


def lane(x, k):
    return jnp.broadcast_to(x[:, k : k + 1], x.shape)


def sublane(x, k):
    return jnp.broadcast_to(x[k : k + 1, :], x.shape)


def tree_sum(terms):
    while len(terms) > 1:
        terms = [
            terms[i] + terms[i + 1] if i + 1 < len(terms) else terms[i]
            for i in range(0, len(terms), 2)
        ]
    return terms[0]


def forward_steps(rows_all, size, found):
    depth = G // 8
    row_ids = lax.broadcasted_iota(jnp.int32, (8, 128), 0)
    before, after = [], []
    for g in range(size // G):
        top, k0 = depth * g, G * g
        rows = list(rows_all[top : top + depth])
        before += rows
        cols = [[lane(rows[h], k0 + j) for h in range(depth)] for j in range(G)]
        for k in range(G):
            kh, ks = divmod(k, 8)
            inverse = 1.0 / sublane(cols[k][kh], ks)
            pivot_row = sublane(rows[kh], ks) * inverse
            pivot_cols = [
                sublane(cols[j][kh], ks) * inverse if j > k else None for j in range(G)
            ]
            factor = cols[k]
            for h in range(depth):
                for j in range(k + 1, G):
                    value = cols[j][h] - factor[h] * pivot_cols[j]
                    cols[j][h] = (
                        jnp.where(row_ids == ks, pivot_cols[j], value) if h == kh else value
                    )
                value = rows[h] - factor[h] * pivot_row
                rows[h] = jnp.where(row_ids == ks, pivot_row, value) if h == kh else value
            yield
        after += rows
        for u in range(top + depth, size // 8):
            rows_all[u] = rows_all[u] - tree_sum(
                [
                    lane(rows_all[u], k0 + j) * sublane(rows[j // 8], j % 8)
                    for j in range(G)
                ]
            )
    found.append((before, after))


def half_inverses(blocks):
    size = blocks[0].shape[0]
    r = lax.broadcasted_iota(jnp.int32, (size, size), 0)
    c = lax.broadcasted_iota(jnp.int32, (size, size), 1)
    eye = jnp.where(r == c, 1.0, 0.0).astype(F32)
    found, steps = [], []
    for block in blocks:
        wide = jnp.concatenate([block, eye], axis=1)
        mine = []
        found.append(mine)
        steps.append(
            forward_steps([wide[8 * i : 8 * i + 8] for i in range(size // 8)], size, mine)
        )
    going = True
    while going:
        for step in steps:
            if next(step, 0) == 0:
                going = False
    out = []
    for mine in found:
        before, after = mine[0]
        out.append(
            (
                jnp.concatenate(before, axis=0)[:, size:],
                jnp.concatenate(after, axis=0)[:, size:],
            )
        )
    return out


def eliminate(diags, bases, between=None):
    upper = [d[:RD] for d in diags]
    lower = list(bases)
    for b in range(3):
        halves = half_inverses([a[:SK, :SK] for a in upper])
        for i, (before, after) in enumerate(halves):
            a, e = upper[i], lower[i]
            z = mm(after, a[:SK, SK:])
            if b < 2:
                upper[i] = a[SK:, SK:] - mm(mm(a[SK:, :SK], before, NT), z)
            lower[i] = e[:, SK:] - mm(mm(e[:, :SK], before, NT), z)
        if between is not None and b < 2:
            between(b)
    return lower


def kernel(
    n_leaf,
    n_col,
    near_h,
    basis_h,
    pb_h,
    gb_h,
    nbr_s,
    live_s,
    leaf_o,
    par_o,
    top_o,
    near_v,
    basis_v,
    pb_v,
    gb_v,
    window,
    turned,
    weigh,
    sent,
    got,
    own_send,
    own_got,
    ring,
    joint,
    mixed,
    mixed_got,
    parts,
    share,
    shares,
    blocks,
    load_sem,
    s_send,
    s_recv,
    f_send,
    f_recv,
    c_sem,
    m_sem,
    e_send,
    e_recv,
):
    total = n_leaf * n_col
    leaf_total = 2 * total
    row = lax.axis_index("leaf")
    col = lax.axis_index("col")
    me = row * n_col + col
    half = lax.rem(col, 2)
    parent = col // 2

    def place(k):
        n = lax.rem(me + k + total, total)
        return (n // n_col, lax.rem(n, n_col))

    partner = (row, col + 1 - 2 * half)

    loads = [
        pltpu.make_async_copy(basis_h, basis_v, load_sem.at[0]),
        pltpu.make_async_copy(near_h.at[:, 0], near_v.at[:, 0], load_sem.at[1]),
        pltpu.make_async_copy(near_h.at[:, 1:], near_v.at[:, 1:], load_sem.at[2]),
        pltpu.make_async_copy(pb_h, pb_v, load_sem.at[3]),
        pltpu.make_async_copy(gb_h, gb_v, load_sem.at[4]),
    ]
    for load in loads:
        load.start()
    barrier = pltpu.get_barrier_semaphore()
    for k in (1, -1, 2, -2, 3, -3):
        pl.semaphore_signal(barrier, inc=1, device_id=place(k), device_id_type=MESH)
    for k in range(1, n_col):
        pl.semaphore_signal(
            barrier, inc=1, device_id=(row, lax.rem(col + k, n_col)), device_id_type=MESH
        )

    loads[0].wait()
    flipped = []
    for i in range(2):
        t = basis_v[i].T
        flipped.append(t)
        window[3, SK * i : SK * (i + 1), :] = t[RD:, :]

    def pass_on(step, side):
        source = 3 - step if side == 0 else 3 + step
        target = source - 1 if side == 0 else source + 1
        return pltpu.make_async_remote_copy(
            src_ref=window.at[source],
            dst_ref=window.at[target],
            send_sem=s_send.at[side, step],
            recv_sem=s_recv.at[side, step],
            device_id=place(1 if side == 0 else -1),
            device_id_type=MESH,
        )

    pl.semaphore_wait(barrier, 6 + n_col - 1)
    hops = [[pass_on(step, side) for side in range(2)] for step in range(3)]
    hops[0][0].start()
    hops[0][1].start()

    loads[1].wait()
    diags = []
    for i in range(2):
        t = mm(flipped[i], near_v[i, 0])
        turned[i, 3, SK * i : SK * (i + 1), :] = t[RD:, :]
        diags.append(mm(t, basis_v[i]))

    def relay(b):
        for side in range(2):
            hops[b][side].wait_recv()
            hops[b + 1][side].start()

    weights = eliminate(diags, [basis_v[0], basis_v[1]], relay)

    slots, lives = [], []
    for i in range(2):
        spots = []
        for q in range(NB):
            away = nbr_s[i, q] - (2 * me + i) + leaf_total + leaf_total // 2
            spot = lax.rem(away, leaf_total) - leaf_total // 2 + 6
            spots.append(jnp.clip(spot, 0, NB - 1))
        found, alive = [], []
        for o in range(NB):
            slot = jnp.int32(0)
            for q in range(1, NB):
                slot = jnp.where(spots[q] == o, q, slot)
            found.append(slot)
            alive.append(live_s[i, slot].astype(F32))
        slots.append((found, spots))
        lives.append(alive)

    loads[2].wait()

    def turn(e):
        for i in range(2):
            for j in range(2):
                o = 2 * (e - 3) + j - i + 6
                at = pl.ds(SK * j, SK)
                if o == 6:
                    continue
                if 0 <= o < NB:
                    turned[i, e, at, :] = (
                        mm(window[e, at, :], near_v[i, slots[i][0][o]]) * lives[i][o]
                    )
                else:
                    turned[i, e, at, :] = jnp.zeros((SK, M), F32)

    v, vt = [], []
    for i in range(2):
        v.append(weights[i] - 0.5 * basis_v[i, :, RD:])
        vt.append(v[i].T)

    def send(e):
        return pltpu.make_async_remote_copy(
            src_ref=sent.at[e],
            dst_ref=got.at[6 - e],
            send_sem=f_send.at[e],
            recv_sem=f_recv.at[6 - e],
            device_id=place(e - 3),
            device_id_type=MESH,
        )

    def out_and_mine(e):
        sent[e] = jnp.concatenate([mm(turned[i, e], v[i]) for i in range(2)], axis=1)
        for i in range(2):
            ring[e + 4, SK * i : SK * (i + 1), :] = mm(vt[i], turned[i, e], NT)

    sends = {e: send(e) for e in range(7) if e != 3}
    turn(3)
    out_and_mine(3)
    mine = ring[7] + sent[3]
    for i in range(2):
        at = slice(SK * i, SK * (i + 1))
        own_send[at, :] = mine[at, :]
        own_send[at, at] = mm(turned[i, 3, at, :], weights[i])
    ring[7] = own_send[...]
    own_copy = pltpu.make_async_remote_copy(
        src_ref=own_send,
        dst_ref=own_got,
        send_sem=c_sem.at[0],
        recv_sem=c_sem.at[1],
        device_id=partner,
        device_id_type=MESH,
    )
    own_copy.start()
    for e in (2, 4):
        turn(e)
        out_and_mine(e)
        sends[e].start()
    for e in (1, 5):
        turn(e)
        out_and_mine(e)
        sends[e].start()
    for side in range(2):
        hops[2][side].wait_recv()
    for e in (0, 6):
        turn(e)
        out_and_mine(e)
        sends[e].start()

    for e in range(4):
        ring[e] = jnp.zeros((128, 128), F32)
        ring[e + 11] = jnp.zeros((128, 128), F32)
    loads[3].wait()
    loads[4].wait()
    pb_own = pb_v[parent]
    pb_flip = pb_own.T
    own_copy.wait_recv()
    for e in (2, 4):
        sends[6 - e].wait_recv()
        ring[e + 4] += got[e]
    cross = ring[8 - 2 * half]
    here = pl.multiple_of(half * 128, 128)
    there = pl.multiple_of(128 - half * 128, 128)
    joint[pl.ds(here, 128), pl.ds(here, 128)] = own_send[...]
    joint[pl.ds(there, 128), pl.ds(there, 128)] = own_got[...]
    joint[pl.ds(here, 128), pl.ds(there, 128)] = cross
    joint[pl.ds(there, 128), pl.ds(here, 128)] = cross.T
    diag = mm(mm(pb_flip, joint[...]), pb_own)

    mixed_copy = pltpu.make_async_remote_copy(
        src_ref=mixed.at[1 - half],
        dst_ref=mixed_got,
        send_sem=m_sem.at[0],
        recv_sem=m_sem.at[1],
        device_id=partner,
        device_id_type=MESH,
    )

    def mix(b):
        if b != 1:
            return
        for e in (1, 5, 0, 6):
            sends[6 - e].wait_recv()
            ring[e + 4] += got[e]
        for u in range(4):
            skel = pb_v[u, :, RD:]
            mixed[u // 2, :, SK * (u % 2) : SK * (u % 2 + 1)] = mm(
                ring[2 * u + 7 - col], skel[:128]
            ) + mm(ring[2 * u + 8 - col], skel[128:])
        mixed_copy.start()

    (w,) = eliminate([diag], [pb_own], mix)
    parts[...] = jnp.concatenate([w - 0.5 * pb_own[:, RD:], 0.5 * w], axis=1)
    mixed_copy.wait_recv()
    both = mm(parts[pl.ds(here, 128), :], mixed[half], TN) + mm(
        parts[pl.ds(there, 128), :], mixed_got[...], TN
    )
    of = lax.broadcasted_iota(jnp.int32, (SK, 128), 1) // SK + 2 * half
    piece = jnp.where(of == parent, both[SK:], both[:SK])
    share[...] = piece
    spreads = []
    for k in range(1, n_col):
        spreads.append(
            pltpu.make_async_remote_copy(
                src_ref=share,
                dst_ref=shares.at[col],
                send_sem=e_send.at[k - 1],
                recv_sem=e_recv.at[k - 1],
                device_id=(row, lax.rem(col + k, n_col)),
                device_id_type=MESH,
            )
        )
    for spread in spreads:
        spread.start()
    shares[col] = piece

    for e in range(7):
        whole = ring[e + 4]
        for i in range(2):
            for j in range(2):
                o = 2 * (e - 3) + j - i + 6
                if 0 <= o < NB:
                    blocks[i, o] = whole[SK * i : SK * (i + 1), SK * j : SK * (j + 1)]
    for i in range(2):
        for q in range(NB):
            spot = slots[i][1][q] if q else 6
            leaf_o[i, :, SK * q : SK * (q + 1)] = blocks[i, spot]

    gb = gb_v[0]
    gb_flip = gb.T
    for k in range(1, n_col):
        pltpu.make_async_remote_copy(
            src_ref=share,
            dst_ref=shares.at[lax.rem(col - k + n_col, n_col)],
            send_sem=e_send.at[k - 1],
            recv_sem=e_recv.at[k - 1],
            device_id=(row, lax.rem(col + k, n_col)),
            device_id_type=MESH,
        ).wait_recv()
    rows = [jnp.concatenate([shares[2 * p], shares[2 * p + 1]], axis=1) for p in range(4)]
    summed = jnp.concatenate(rows, axis=0)
    summed = summed + summed.T
    for p in range(4):
        par_o[p] = summed[SK * p : SK * (p + 1)]
    t = mm(gb_flip, summed)
    (w,) = eliminate([mm(t, gb)], [gb])
    top_o[0] = mm(t[RD:], w)

    for step in range(3):
        for side in range(2):
            hops[step][side].wait_send()
    for e in sends:
        sends[e].wait_send()
    own_copy.wait_send()
    mixed_copy.wait_send()
    for spread in spreads:
        spread.wait_send()


def on_device(n_leaf, n_col, near, basis, parent_basis, grand_basis, nbr, live, partner):
    hbm = pl.BlockSpec(memory_space=pl.ANY)
    smem = pl.BlockSpec(memory_space=pltpu.SMEM)
    vmem = pl.BlockSpec(memory_space=pltpu.VMEM)
    dma = pltpu.SemaphoreType.DMA
    return pl.pallas_call(
        functools.partial(kernel, n_leaf, n_col),
        out_shape=(
            jax.ShapeDtypeStruct((2, SK, NB * SK), F32),
            jax.ShapeDtypeStruct((4, SK, M), F32),
            jax.ShapeDtypeStruct((1, SK, SK), F32),
        ),
        in_specs=[hbm, hbm, hbm, hbm, smem, smem],
        out_specs=(vmem, vmem, vmem),
        scratch_shapes=[
            pltpu.VMEM((2, NB, M, M), F32),
            pltpu.VMEM((2, M, M), F32),
            pltpu.VMEM((4, M, M), F32),
            pltpu.VMEM((1, M, M), F32),
            pltpu.VMEM((7, 128, M), F32),
            pltpu.VMEM((2, 7, 128, M), F32),
            pltpu.VMEM((8, 128), F32),
            pltpu.VMEM((7, 128, 128), F32),
            pltpu.VMEM((7, 128, 128), F32),
            pltpu.VMEM((128, 128), F32),
            pltpu.VMEM((128, 128), F32),
            pltpu.VMEM((15, 128, 128), F32),
            pltpu.VMEM((M, M), F32),
            pltpu.VMEM((2, 128, 128), F32),
            pltpu.VMEM((128, 128), F32),
            pltpu.VMEM((M, 128), F32),
            pltpu.VMEM((SK, 128), F32),
            pltpu.VMEM((8, SK, 128), F32),
            pltpu.VMEM((2, NB, SK, SK), F32),
            dma((5,)),
            dma((2, 3)),
            dma((2, 3)),
            dma((7,)),
            dma((7,)),
            dma((2,)),
            dma((2,)),
            dma((7,)),
            dma((7,)),
        ],
        compiler_params=pltpu.CompilerParams(
            collective_id=0, has_side_effects=True, vmem_limit_bytes=50 * 1024 * 1024
        ),
    )(near, basis, parent_basis, grand_basis, nbr, live)


def solution(mesh):
    both = ("leaf", "col")
    return jax.shard_map(
        functools.partial(on_device, mesh.shape["leaf"], mesh.shape["col"]),
        mesh=mesh,
        in_specs=(
            P(both, None, None, None),
            P(both, None, None),
            P("leaf", None, None),
            P("leaf", None, None),
            P(both, None),
            P(both, None),
            P(both, None),
        ),
        out_specs=(P(both, None, None), P("leaf", None, None), P("leaf", None, None)),
        check_vma=False,
    )
```

time: 735 us -> 67.5 us (0.09); the launches traced: 721 us -> 66.6 us
  other arithmetic: 352 us -> 0 us
  waiting for transfers between devices: 204 us -> 0 us
  matrix products: 61.2 us -> 0 us
  Pallas kernels: 0 us -> 59.3 us
  local copies, waits for them, and re-layouts: 60.5 us -> 6.65 us
  starting transfers between devices: 26.6 us -> 0 us
  between operations: 16.7 us -> 0.65 us
    another operation x41 -> x0, other arithmetic: 347 us -> none  [the longest x25 200 us: eliminate(): factor = jnp.linalg.cholesky(diag_block[:, :redundant, :redundant])]
    ppermute x12 -> x0, waiting for transfers between devices: 146 us -> none  [shifted(): return lax.ppermute(value, axis, pairs)]
    pallas_call x0 -> x1, Pallas kernels: none -> 59.3 us  [on_device(): pl.pallas_call(functools.partial(kernel, n_leaf, n_col), out_shape=(jax.S...]
    all_gather x1 -> x0, waiting for transfers between devices: 58.7 us -> none  [on_device(): all_rows = lax.all_gather(grand_rows, 'col', axis=0, tiled=True)]
    dot_general x14 -> x0, matrix products: 45.9 us -> none  [the longest x1 10.8 us: parent_level(): jnp.einsum('nab,nac->nbc', own_basis, stacked, precision=FULL_PRECISION)]
    ppermute x12 -> x0, starting transfers between devices: 26.5 us -> none  [shifted(): return lax.ppermute(value, axis, pairs)]
    another operation x24 -> x0, matrix products: 15.3 us -> none  [the longest x18 10.3 us: eliminate(): jax.scipy.linalg.cho_solve((factor, True), diag_block[:, :redundant, redu...]
    concatenate x3 -> x0, local copies, waits for them, and re-layouts: 14.4 us -> none  [the longest x2 14.2 us: reply_window(): return jnp.concatenate(below_list[::-1] + [replies] + above_list, axis=0)]
  transfers between devices with their start and end apart: 13 -> 0, of which waited for: 8 -> 0; matrix products, arithmetic and copies ran while one was open for 18% -> 0% of each run, Pallas kernels for 0% -> 0%
where the time goes in v1:
time: 67.5 us; the launch traced here: 66.6 us
  Pallas kernels  59.3 us (88%)
  local copies, waits for them, and re-layouts  6.65 us (10%)
    pallas_call x1, Pallas kernels, on_device(): pl.pallas_call(functools.partial(kernel, n_leaf, n_col), out_shape=(jax.S...  59.3 us
    unnamed x13, local copies, waits for them, and re-layouts  6.65 us

profile of v1, /device:TPU:32, one launch (start us, length us, event | category | flops | bytes accessed | tf_op | source)
XLA Modules:
  0.0 66.6 jit_solution(9280472895702392636)
XLA Ops:
  0.6 0.0 copy-start
  0.6 1.2 %copy-done = f32[4,256,256]{2,1,0:T(8,128)S(1)} copy-done((f32[4,256,256]{2,1,0:T(8,128)S(1)}, f32[4,256,256]{2,1,0:T(8,128)}, u32[]{:S(2)}) %copy-start) | copy-done | bytes 1048600
  1.9 0.0 copy-start.1
  1.9 1.0 %copy-done.1 = f32[2,256,256]{2,1,0:T(8,128)S(1)} copy-done((f32[2,256,256]{2,1,0:T(8,128)S(1)}, f32[2,256,256]{2,1,0:T(8,128)}, u32[]{:S(2)}) %copy-start.1) | copy-done | bytes 524312
  2.9 0.0 copy-start.2
  2.9 0.9 %copy-done.2 = f32[1,256,256]{2,1,0:T(8,128)S(1)} copy-done((f32[1,256,256]{2,1,0:T(8,128)S(1)}, f32[1,256,256]{2,1,0:T(8,128)}, u32[]{:S(2)}) %copy-start.2) | copy-done | bytes 262168
  3.9 0.0 copy-start.3
  3.9 0.7 %copy-done.3 = s32[2,13]{1,0:T(2,128)S(1)} copy-done((s32[2,13]{1,0:T(2,128)S(1)}, s32[2,13]{1,0:T(2,128)}, u32[]{:S(2)}) %copy-start.3) | copy-done | bytes 128
  4.5 0.0 copy-start.4
  4.5 0.7 %copy-done.4 = s32[2,13]{1,0:T(2,128)S(1)} copy-done((s32[2,13]{1,0:T(2,128)S(1)}, s32[2,13]{1,0:T(2,128)}, u32[]{:S(2)}) %copy-start.4) | copy-done | bytes 128
  5.2 59.3 %shard_map.85 = (f32[2,64,832]{2,1,0:T(8,128)S(1)}, f32[4,64,256]{2,1,0:T(8,128)S(1)}, f32[1,64,64]{2,1,0:T(8,128)S(1)}) custom-call(f32[2,13,256,256]{3,2,1,0:T(8,128)} %near_h.1, f32[2,256,256]{2,1,0:T(8,128)S(1)} %copy-done.1, f32[4,256,256]{2,1,0:T(8,128)S(1)} %copy-done, f32[1,256,256]{2,1,0:T(8,128)S(1)} %copy-done.2, s32[2,13]{1,0:T(2,128)S(1)} %copy-done.3, ...), custom_call_target="tpu_custom_call" | custom-call | tf_op jit(solution)/shard_map/pallas_call | solution.py:438
  64.5 0.8 %copy.12 = f32[2,64,832]{2,1,0:T(8,128)} copy(f32[2,64,832]{2,1,0:T(8,128)S(1)} %get-tuple-element.6) | data formatting | bytes 851968
  65.3 0.7 %copy.13 = f32[4,64,256]{2,1,0:T(8,128)} copy(f32[4,64,256]{2,1,0:T(8,128)S(1)} %get-tuple-element.7) | data formatting | bytes 524288
  66.0 0.6 copy.14
Async XLA Ops:
  0.6 1.2 %copy-start = (f32[4,256,256]{2,1,0:T(8,128)S(1)}, f32[4,256,256]{2,1,0:T(8,128)}, u32[]{:S(2)}) copy-start(f32[4,256,256]{2,1,0:T(8,128)} %pb_h.1) | copy-start | bytes 3145732
  1.9 1.0 %copy-start.1 = (f32[2,256,256]{2,1,0:T(8,128)S(1)}, f32[2,256,256]{2,1,0:T(8,128)}, u32[]{:S(2)}) copy-start(f32[2,256,256]{2,1,0:T(8,128)} %basis_h.1) | copy-start | bytes 1572868
  2.9 0.9 %copy-start.2 = (f32[1,256,256]{2,1,0:T(8,128)S(1)}, f32[1,256,256]{2,1,0:T(8,128)}, u32[]{:S(2)}) copy-start(f32[1,256,256]{2,1,0:T(8,128)} %gb_h.1) | copy-start | bytes 786436
  3.9 0.7 %copy-start.3 = (s32[2,13]{1,0:T(2,128)S(1)}, s32[2,13]{1,0:T(2,128)}, u32[]{:S(2)}) copy-start(s32[2,13]{1,0:T(2,128)} %nbr_s.1) | copy-start | bytes 316
  4.5 0.7 %copy-start.4 = (s32[2,13]{1,0:T(2,128)S(1)}, s32[2,13]{1,0:T(2,128)}, u32[]{:S(2)}) copy-start(s32[2,13]{1,0:T(2,128)} %live_s.1) | copy-start | bytes 316

commit v2 on v1

--- a/solution.py
+++ b/solution.py
@@ -15,6 +15,7 @@
 F32 = jnp.float32
 HIGH = lax.Precision.HIGH
 MESH = pl.DeviceIdType.MESH
+VMEM_ALL = 67_000_000
 NN = ((1,), (0,))
 NT = ((1,), (1,))
 TN = ((0,), (0,))
@@ -49,32 +50,35 @@
         top, k0 = depth * g, G * g
         rows = list(rows_all[top : top + depth])
         before += rows
+        following = range(top + depth, min(top + 2 * depth, size // 8))
+        later = range(top + 2 * depth, size // 8)
+        ahead = {u: [lane(rows_all[u], k0 + j) for j in range(G)] for u in following}
         cols = [[lane(rows[h], k0 + j) for h in range(depth)] for j in range(G)]
+        scale = [None] * depth
         for k in range(G):
             kh, ks = divmod(k, 8)
             inverse = 1.0 / sublane(cols[k][kh], ks)
-            pivot_row = sublane(rows[kh], ks) * inverse
-            pivot_cols = [
-                sublane(cols[j][kh], ks) * inverse if j > k else None for j in range(G)
-            ]
-            factor = cols[k]
-            for h in range(depth):
-                for j in range(k + 1, G):
-                    value = cols[j][h] - factor[h] * pivot_cols[j]
-                    cols[j][h] = (
-                        jnp.where(row_ids == ks, pivot_cols[j], value) if h == kh else value
-                    )
-                value = rows[h] - factor[h] * pivot_row
-                rows[h] = jnp.where(row_ids == ks, pivot_row, value) if h == kh else value
+            here = row_ids == ks
+            scale[kh] = inverse if ks == 0 else jnp.where(here, inverse, scale[kh])
+            factor = [c * inverse for c in cols[k]]
+            factor[kh] = jnp.where(here, 0.0, factor[kh])
+            for j in range(k + 1, G):
+                pivot = sublane(cols[j][kh], ks)
+                cols[j] = [cols[j][h] - factor[h] * pivot for h in range(depth)]
+            pivot = sublane(rows[kh], ks)
+            rows = [rows[h] - factor[h] * pivot for h in range(depth)]
             yield
+        rows = [rows[h] * scale[h] for h in range(depth)]
         after += rows
-        for u in range(top + depth, size // 8):
+        for u in following:
             rows_all[u] = rows_all[u] - tree_sum(
-                [
-                    lane(rows_all[u], k0 + j) * sublane(rows[j // 8], j % 8)
-                    for j in range(G)
-                ]
+                [ahead[u][j] * sublane(rows[j // 8], j % 8) for j in range(G)]
             )
+        if later:
+            left = jnp.concatenate([rows_all[u] for u in later], axis=0)[:, k0 : k0 + G]
+            change = mm(left, jnp.concatenate(rows, axis=0))
+            for n, u in enumerate(later):
+                rows_all[u] = rows_all[u] - change[8 * n : 8 * n + 8]
     found.append((before, after))
 
 
@@ -130,19 +134,15 @@
     near_h,
     basis_h,
     pb_h,
-    gb_h,
-    nbr_s,
-    live_s,
-    leaf_o,
-    par_o,
-    top_o,
+    nbr_h,
+    live_h,
+    ring_o,
+    joined_o,
     near_v,
     basis_v,
     pb_v,
-    gb_v,
     window,
     turned,
-    weigh,
     sent,
     got,
     own_send,
@@ -154,7 +154,9 @@
     parts,
     share,
     shares,
-    blocks,
+    joined,
+    nbr_s,
+    live_s,
     load_sem,
     s_send,
     s_recv,
@@ -164,6 +166,7 @@
     m_sem,
     e_send,
     e_recv,
+    save_sem,
 ):
     total = n_leaf * n_col
     leaf_total = 2 * total
@@ -180,11 +183,12 @@
     partner = (row, col + 1 - 2 * half)
 
     loads = [
+        pltpu.make_async_copy(nbr_h, nbr_s, load_sem.at[4]),
+        pltpu.make_async_copy(live_h, live_s, load_sem.at[5]),
         pltpu.make_async_copy(basis_h, basis_v, load_sem.at[0]),
         pltpu.make_async_copy(near_h.at[:, 0], near_v.at[:, 0], load_sem.at[1]),
         pltpu.make_async_copy(near_h.at[:, 1:], near_v.at[:, 1:], load_sem.at[2]),
         pltpu.make_async_copy(pb_h, pb_v, load_sem.at[3]),
-        pltpu.make_async_copy(gb_h, gb_v, load_sem.at[4]),
     ]
     for load in loads:
         load.start()
@@ -196,7 +200,7 @@
             barrier, inc=1, device_id=(row, lax.rem(col + k, n_col)), device_id_type=MESH
         )
 
-    loads[0].wait()
+    loads[2].wait()
     flipped = []
     for i in range(2):
         t = basis_v[i].T
@@ -220,20 +224,15 @@
     hops[0][0].start()
     hops[0][1].start()
 
-    loads[1].wait()
+    loads[3].wait()
     diags = []
     for i in range(2):
         t = mm(flipped[i], near_v[i, 0])
         turned[i, 3, SK * i : SK * (i + 1), :] = t[RD:, :]
         diags.append(mm(t, basis_v[i]))
 
-    def relay(b):
-        for side in range(2):
-            hops[b][side].wait_recv()
-            hops[b + 1][side].start()
-
-    weights = eliminate(diags, [basis_v[0], basis_v[1]], relay)
-
+    loads[0].wait()
+    loads[1].wait()
     slots, lives = [], []
     for i in range(2):
         spots = []
@@ -251,7 +250,7 @@
         slots.append((found, spots))
         lives.append(alive)
 
-    loads[2].wait()
+    loads[4].wait()
 
     def turn(e):
         for i in range(2):
@@ -267,6 +266,20 @@
                 else:
                     turned[i, e, at, :] = jnp.zeros((SK, M), F32)
 
+    def relay(b):
+        for side in range(2):
+            hops[b][side].wait_recv()
+            hops[b + 1][side].start()
+
+    def early(b):
+        if b == 1:
+            relay(0)
+            turn(3)
+            turn(2)
+            turn(4)
+
+    weights = eliminate(diags, [basis_v[0], basis_v[1]], early)
+
     v, vt = [], []
     for i in range(2):
         v.append(weights[i] - 0.5 * basis_v[i, :, RD:])
@@ -288,7 +301,6 @@
             ring[e + 4, SK * i : SK * (i + 1), :] = mm(vt[i], turned[i, e], NT)
 
     sends = {e: send(e) for e in range(7) if e != 3}
-    turn(3)
     out_and_mine(3)
     mine = ring[7] + sent[3]
     for i in range(2):
@@ -306,9 +318,9 @@
     )
     own_copy.start()
     for e in (2, 4):
-        turn(e)
         out_and_mine(e)
         sends[e].start()
+    relay(1)
     for e in (1, 5):
         turn(e)
         out_and_mine(e)
@@ -323,8 +335,7 @@
     for e in range(4):
         ring[e] = jnp.zeros((128, 128), F32)
         ring[e + 11] = jnp.zeros((128, 128), F32)
-    loads[3].wait()
-    loads[4].wait()
+    loads[5].wait()
     pb_own = pb_v[parent]
     pb_flip = pb_own.T
     own_copy.wait_recv()
@@ -383,24 +394,12 @@
                 device_id_type=MESH,
             )
         )
-    for spread in spreads:
-        spread.start()
+    for k in (4, 3, 5, 2, 6, 1, 7):
+        spreads[k - 1].start()
     shares[col] = piece
-
-    for e in range(7):
-        whole = ring[e + 4]
-        for i in range(2):
-            for j in range(2):
-                o = 2 * (e - 3) + j - i + 6
-                if 0 <= o < NB:
-                    blocks[i, o] = whole[SK * i : SK * (i + 1), SK * j : SK * (j + 1)]
-    for i in range(2):
-        for q in range(NB):
-            spot = slots[i][1][q] if q else 6
-            leaf_o[i, :, SK * q : SK * (q + 1)] = blocks[i, spot]
-
-    gb = gb_v[0]
-    gb_flip = gb.T
+    ring_save = pltpu.make_async_copy(ring.at[4:11], ring_o, save_sem.at[0])
+    ring_save.start()
+
     for k in range(1, n_col):
         pltpu.make_async_remote_copy(
             src_ref=share,
@@ -412,12 +411,9 @@
         ).wait_recv()
     rows = [jnp.concatenate([shares[2 * p], shares[2 * p + 1]], axis=1) for p in range(4)]
     summed = jnp.concatenate(rows, axis=0)
-    summed = summed + summed.T
-    for p in range(4):
-        par_o[p] = summed[SK * p : SK * (p + 1)]
-    t = mm(gb_flip, summed)
-    (w,) = eliminate([mm(t, gb)], [gb])
-    top_o[0] = mm(t[RD:], w)
+    joined[...] = summed + summed.T
+    joined_save = pltpu.make_async_copy(joined, joined_o, save_sem.at[1])
+    joined_save.start()
 
     for step in range(3):
         for side in range(2):
@@ -428,30 +424,88 @@
     mixed_copy.wait_send()
     for spread in spreads:
         spread.wait_send()
+    ring_save.wait()
+    joined_save.wait()
+
+
+def finish(
+    n_leaf,
+    n_col,
+    ring_h,
+    joined_h,
+    gb_h,
+    nbr_h,
+    leaf_o,
+    par_o,
+    top_o,
+    ring,
+    joined,
+    gb_v,
+    nbr_s,
+    blocks,
+    leaf_v,
+    load_sem,
+    leaf_sem,
+    par_sem,
+):
+    leaf_total = 2 * n_leaf * n_col
+    me = lax.axis_index("leaf") * n_col + lax.axis_index("col")
+    loads = [
+        pltpu.make_async_copy(gb_h, gb_v, load_sem.at[0]),
+        pltpu.make_async_copy(joined_h, joined, load_sem.at[1]),
+        pltpu.make_async_copy(nbr_h, nbr_s, load_sem.at[2]),
+        pltpu.make_async_copy(ring_h, ring, load_sem.at[3]),
+    ]
+    for load in loads:
+        load.start()
+    for load in loads:
+        load.wait()
+    saves = [
+        pltpu.make_async_copy(joined.at[pl.ds(SK * p, SK)], par_o.at[p], par_sem.at[p])
+        for p in range(4)
+    ]
+    for save in saves:
+        save.start()
+    for e in range(7):
+        whole = ring[e]
+        for i in range(2):
+            for j in range(2):
+                o = 2 * (e - 3) + j - i + 6
+                if 0 <= o < NB:
+                    blocks[i, o] = whole[SK * i : SK * (i + 1), SK * j : SK * (j + 1)]
+    for i in range(2):
+        for q in range(NB):
+            away = nbr_s[i, q] - (2 * me + i) + leaf_total + leaf_total // 2
+            spot = lax.rem(away, leaf_total) - leaf_total // 2 + 6
+            leaf_v[i, :, SK * q : SK * (q + 1)] = blocks[i, jnp.clip(spot, 0, NB - 1)]
+    saves.append(pltpu.make_async_copy(leaf_v, leaf_o, leaf_sem))
+    saves[-1].start()
+    gb = gb_v[0]
+    t = mm(gb.T, joined[...])
+    (w,) = eliminate([mm(t, gb)], [gb])
+    top_o[0] = mm(t[RD:], w)
+    for save in saves:
+        save.wait()
 
 
 def on_device(n_leaf, n_col, near, basis, parent_basis, grand_basis, nbr, live, partner):
-    hbm = pl.BlockSpec(memory_space=pl.ANY)
-    smem = pl.BlockSpec(memory_space=pltpu.SMEM)
+    hbm = pl.BlockSpec(memory_space=pltpu.HBM)
     vmem = pl.BlockSpec(memory_space=pltpu.VMEM)
     dma = pltpu.SemaphoreType.DMA
-    return pl.pallas_call(
+    ring, joined = pl.pallas_call(
         functools.partial(kernel, n_leaf, n_col),
         out_shape=(
-            jax.ShapeDtypeStruct((2, SK, NB * SK), F32),
-            jax.ShapeDtypeStruct((4, SK, M), F32),
-            jax.ShapeDtypeStruct((1, SK, SK), F32),
+            jax.ShapeDtypeStruct((7, 128, 128), F32),
+            jax.ShapeDtypeStruct((M, M), F32),
         ),
-        in_specs=[hbm, hbm, hbm, hbm, smem, smem],
-        out_specs=(vmem, vmem, vmem),
+        in_specs=[hbm] * 5,
+        out_specs=(hbm, hbm),
         scratch_shapes=[
             pltpu.VMEM((2, NB, M, M), F32),
             pltpu.VMEM((2, M, M), F32),
             pltpu.VMEM((4, M, M), F32),
-            pltpu.VMEM((1, M, M), F32),
             pltpu.VMEM((7, 128, M), F32),
             pltpu.VMEM((2, 7, 128, M), F32),
-            pltpu.VMEM((8, 128), F32),
             pltpu.VMEM((7, 128, 128), F32),
             pltpu.VMEM((7, 128, 128), F32),
             pltpu.VMEM((128, 128), F32),
@@ -463,8 +517,10 @@
             pltpu.VMEM((M, 128), F32),
             pltpu.VMEM((SK, 128), F32),
             pltpu.VMEM((8, SK, 128), F32),
-            pltpu.VMEM((2, NB, SK, SK), F32),
-            dma((5,)),
+            pltpu.VMEM((M, M), F32),
+            pltpu.SMEM((2, NB), jnp.int32),
+            pltpu.SMEM((2, NB), jnp.int32),
+            dma((6,)),
             dma((2, 3)),
             dma((2, 3)),
             dma((7,)),
@@ -473,11 +529,34 @@
             dma((2,)),
             dma((7,)),
             dma((7,)),
+            dma((2,)),
         ],
         compiler_params=pltpu.CompilerParams(
-            collective_id=0, has_side_effects=True, vmem_limit_bytes=50 * 1024 * 1024
+            collective_id=0, has_side_effects=True, vmem_limit_bytes=VMEM_ALL
         ),
-    )(near, basis, parent_basis, grand_basis, nbr, live)
+    )(near, basis, parent_basis, nbr, live)
+    return pl.pallas_call(
+        functools.partial(finish, n_leaf, n_col),
+        out_shape=(
+            jax.ShapeDtypeStruct((2, SK, NB * SK), F32),
+            jax.ShapeDtypeStruct((4, SK, M), F32),
+            jax.ShapeDtypeStruct((1, SK, SK), F32),
+        ),
+        in_specs=[hbm] * 4,
+        out_specs=(hbm, hbm, vmem),
+        scratch_shapes=[
+            pltpu.VMEM((7, 128, 128), F32),
+            pltpu.VMEM((M, M), F32),
+            pltpu.VMEM((1, M, M), F32),
+            pltpu.SMEM((2, NB), jnp.int32),
+            pltpu.VMEM((2, NB, SK, SK), F32),
+            pltpu.VMEM((2, SK, NB * SK), F32),
+            dma((4,)),
+            dma(()),
+            dma((4,)),
+        ],
+        compiler_params=pltpu.CompilerParams(vmem_limit_bytes=VMEM_ALL),
+    )(ring, joined, grand_basis, nbr)
 
 
 def solution(mesh):

time: 67.5 us -> 59.5 us (0.88); the launches traced: 66.6 us -> 59.4 us
  local copies, waits for them, and re-layouts: 6.65 us -> 0 us
  Pallas kernels: 59.3 us -> 58.6 us
    pallas_call x1, Pallas kernels: 59.3 us -> 49.4 us  [on_device(): pl.pallas_call(functools.partial(kernel, n_leaf, n_col), out_shape=(jax.S...]
    pallas_call x0 -> x1, Pallas kernels: none -> 9.16 us  [on_device(): pl.pallas_call(functools.partial(finish, n_leaf, n_col), out_shape=(jax.S...]
    unnamed x13 -> x0, local copies, waits for them, and re-layouts: 6.65 us -> none
where the time goes in v2:
time: 59.5 us; the launch traced here: 59.4 us
  Pallas kernels  58.6 us (98%)
  between operations  0.8 us (1%)
    pallas_call x1, Pallas kernels, on_device(): pl.pallas_call(functools.partial(kernel, n_leaf, n_col), out_shape=(jax.S...  49.4 us
    pallas_call x1, Pallas kernels, on_device(): pl.pallas_call(functools.partial(finish, n_leaf, n_col), out_shape=(jax.S...  9.16 us

profile of v2, /device:TPU:32, one launch (start us, length us, event | category | flops | bytes accessed | tf_op | source)
XLA Modules:
  0.0 59.4 jit_solution(303567751404391301)
XLA Ops:
  0.6 49.4 %shard_map.85 = (f32[7,128,128]{2,1,0:T(8,128)}, f32[256,256]{1,0:T(8,128)}) custom-call(f32[2,13,256,256]{3,2,1,0:T(8,128)} %near_h.1, f32[2,256,256]{2,1,0:T(8,128)} %basis_h.1, f32[4,256,256]{2,1,0:T(8,128)} %pb_h.1, s32[2,13]{1,0:T(2,128)} %nbr_h.3, s32[2,13]{1,0:T(2,128)} %live_h.1), custom_call_target="tpu_custom_call" | custom-call | tf_op jit(solution)/shard_map/pallas_call | solution.py:495
  50.1 9.2 %shard_map.86 = (f32[2,64,832]{2,1,0:T(8,128)}, f32[4,64,256]{2,1,0:T(8,128)}, f32[1,64,64]{2,1,0:T(8,128)}) custom-call(f32[7,128,128]{2,1,0:T(8,128)} %get-tuple-element.5.ring_h, f32[256,256]{1,0:T(8,128)} %get-tuple-element.6.joined_h, f32[1,256,256]{2,1,0:T(8,128)} %gb_h.1, s32[2,13]{1,0:T(2,128)} %nbr_h.3), custom_call_target="tpu_custom_call" | custom-call | tf_op jit(solution)/shard_map/pallas_call | solution.py:538

commit v3 on v2

--- a/solution.py
+++ b/solution.py
@@ -166,6 +166,7 @@
     m_sem,
     e_send,
     e_recv,
+    r_sem,
     save_sem,
 ):
     total = n_leaf * n_col
@@ -201,28 +202,28 @@
         )
 
     loads[2].wait()
-    flipped = []
     for i in range(2):
-        t = basis_v[i].T
-        flipped.append(t)
-        window[3, SK * i : SK * (i + 1), :] = t[RD:, :]
-
-    def pass_on(step, side):
+        window[3, SK * i : SK * (i + 1), :] = basis_v[i, :, RD:].T
+
+    def pass_on(step, side, j):
         source = 3 - step if side == 0 else 3 + step
         target = source - 1 if side == 0 else source + 1
         return pltpu.make_async_remote_copy(
-            src_ref=window.at[source],
-            dst_ref=window.at[target],
-            send_sem=s_send.at[side, step],
-            recv_sem=s_recv.at[side, step],
+            src_ref=window.at[source, pl.ds(SK * j, SK)],
+            dst_ref=window.at[target, pl.ds(SK * j, SK)],
+            send_sem=s_send.at[side, step, j],
+            recv_sem=s_recv.at[side, step, j],
             device_id=place(1 if side == 0 else -1),
             device_id_type=MESH,
         )
 
     pl.semaphore_wait(barrier, 6 + n_col - 1)
-    hops = [[pass_on(step, side) for side in range(2)] for step in range(3)]
-    hops[0][0].start()
-    hops[0][1].start()
+    hops = [
+        [pass_on(step, side, j) for j in range(2) for side in range(2)] for step in range(3)
+    ]
+    for hop in hops[0]:
+        hop.start()
+    flipped = [basis_v[i].T for i in range(2)]
 
     loads[3].wait()
     diags = []
@@ -267,9 +268,9 @@
                     turned[i, e, at, :] = jnp.zeros((SK, M), F32)
 
     def relay(b):
-        for side in range(2):
-            hops[b][side].wait_recv()
-            hops[b + 1][side].start()
+        for hop, onward in zip(hops[b], hops[b + 1]):
+            hop.wait_recv()
+            onward.start()
 
     def early(b):
         if b == 1:
@@ -279,6 +280,7 @@
             turn(4)
 
     weights = eliminate(diags, [basis_v[0], basis_v[1]], early)
+    relay(1)
 
     v, vt = [], []
     for i in range(2):
@@ -320,13 +322,12 @@
     for e in (2, 4):
         out_and_mine(e)
         sends[e].start()
-    relay(1)
     for e in (1, 5):
         turn(e)
         out_and_mine(e)
         sends[e].start()
-    for side in range(2):
-        hops[2][side].wait_recv()
+    for hop in hops[2]:
+        hop.wait_recv()
     for e in (0, 6):
         turn(e)
         out_and_mine(e)
@@ -382,33 +383,39 @@
     of = lax.broadcasted_iota(jnp.int32, (SK, 128), 1) // SK + 2 * half
     piece = jnp.where(of == parent, both[SK:], both[:SK])
     share[...] = piece
-    spreads = []
-    for k in range(1, n_col):
-        spreads.append(
-            pltpu.make_async_remote_copy(
-                src_ref=share,
-                dst_ref=shares.at[col],
-                send_sem=e_send.at[k - 1],
-                recv_sem=e_recv.at[k - 1],
-                device_id=(row, lax.rem(col + k, n_col)),
-                device_id_type=MESH,
-            )
-        )
-    for k in (4, 3, 5, 2, 6, 1, 7):
-        spreads[k - 1].start()
-    shares[col] = piece
-    ring_save = pltpu.make_async_copy(ring.at[4:11], ring_o, save_sem.at[0])
-    ring_save.start()
-
-    for k in range(1, n_col):
-        pltpu.make_async_remote_copy(
+    spreads = {}
+    for k in (3, 5, 2, 6, 1, 7):
+        spreads[k] = pltpu.make_async_remote_copy(
             src_ref=share,
-            dst_ref=shares.at[lax.rem(col - k + n_col, n_col)],
+            dst_ref=shares.at[col],
             send_sem=e_send.at[k - 1],
             recv_sem=e_recv.at[k - 1],
             device_id=(row, lax.rem(col + k, n_col)),
             device_id_type=MESH,
-        ).wait_recv()
+        )
+        spreads[k].start()
+    shares[col] = piece
+    ring_save = pltpu.make_async_copy(ring.at[4:11], ring_o, save_sem.at[0])
+    ring_save.start()
+
+    onwards = []
+    for k, step, side in ((3, 1, 0), (5, n_col - 1, 1)):
+        spreads[k].wait_recv()
+        source = lax.rem(col - k + n_col, n_col)
+        onward = pltpu.make_async_remote_copy(
+            src_ref=shares.at[source, pl.ds(32 * side, 32)],
+            dst_ref=shares.at[source, pl.ds(32 * side, 32)],
+            send_sem=r_sem.at[side],
+            recv_sem=r_sem.at[2 + side],
+            device_id=(row, lax.rem(col + step, n_col)),
+            device_id_type=MESH,
+        )
+        onward.start()
+        onwards.append(onward)
+    for k in (2, 6, 1, 7):
+        spreads[k].wait_recv()
+    for onward in onwards:
+        onward.wait_recv()
     rows = [jnp.concatenate([shares[2 * p], shares[2 * p + 1]], axis=1) for p in range(4)]
     summed = jnp.concatenate(rows, axis=0)
     joined[...] = summed + summed.T
@@ -416,14 +423,16 @@
     joined_save.start()
 
     for step in range(3):
-        for side in range(2):
-            hops[step][side].wait_send()
+        for hop in hops[step]:
+            hop.wait_send()
     for e in sends:
         sends[e].wait_send()
     own_copy.wait_send()
     mixed_copy.wait_send()
-    for spread in spreads:
-        spread.wait_send()
+    for k in spreads:
+        spreads[k].wait_send()
+    for onward in onwards:
+        onward.wait_send()
     ring_save.wait()
     joined_save.wait()
 
@@ -458,31 +467,37 @@
     ]
     for load in loads:
         load.start()
-    for load in loads:
-        load.wait()
+    loads[0].wait()
+    loads[1].wait()
     saves = [
         pltpu.make_async_copy(joined.at[pl.ds(SK * p, SK)], par_o.at[p], par_sem.at[p])
         for p in range(4)
     ]
     for save in saves:
         save.start()
-    for e in range(7):
-        whole = ring[e]
+    def tidy(b):
+        if b:
+            return
+        loads[2].wait()
+        loads[3].wait()
+        for e in range(7):
+            whole = ring[e]
+            for i in range(2):
+                for j in range(2):
+                    o = 2 * (e - 3) + j - i + 6
+                    if 0 <= o < NB:
+                        blocks[i, o] = whole[SK * i : SK * (i + 1), SK * j : SK * (j + 1)]
         for i in range(2):
-            for j in range(2):
-                o = 2 * (e - 3) + j - i + 6
-                if 0 <= o < NB:
-                    blocks[i, o] = whole[SK * i : SK * (i + 1), SK * j : SK * (j + 1)]
-    for i in range(2):
-        for q in range(NB):
-            away = nbr_s[i, q] - (2 * me + i) + leaf_total + leaf_total // 2
-            spot = lax.rem(away, leaf_total) - leaf_total // 2 + 6
-            leaf_v[i, :, SK * q : SK * (q + 1)] = blocks[i, jnp.clip(spot, 0, NB - 1)]
-    saves.append(pltpu.make_async_copy(leaf_v, leaf_o, leaf_sem))
-    saves[-1].start()
+            for q in range(NB):
+                away = nbr_s[i, q] - (2 * me + i) + leaf_total + leaf_total // 2
+                spot = lax.rem(away, leaf_total) - leaf_total // 2 + 6
+                leaf_v[i, :, SK * q : SK * (q + 1)] = blocks[i, jnp.clip(spot, 0, NB - 1)]
+        saves.append(pltpu.make_async_copy(leaf_v, leaf_o, leaf_sem))
+        saves[-1].start()
+
     gb = gb_v[0]
     t = mm(gb.T, joined[...])
-    (w,) = eliminate([mm(t, gb)], [gb])
+    (w,) = eliminate([mm(t, gb)], [gb], tidy)
     top_o[0] = mm(t[RD:], w)
     for save in saves:
         save.wait()
@@ -521,14 +536,15 @@
             pltpu.SMEM((2, NB), jnp.int32),
             pltpu.SMEM((2, NB), jnp.int32),
             dma((6,)),
-            dma((2, 3)),
-            dma((2, 3)),
+            dma((2, 3, 2)),
+            dma((2, 3, 2)),
             dma((7,)),
             dma((7,)),
             dma((2,)),
             dma((2,)),
             dma((7,)),
             dma((7,)),
+            dma((4,)),
             dma((2,)),
         ],
         compiler_params=pltpu.CompilerParams(

time: 59.5 us -> 63.6 us (1.069)
  the two profiles are of different devices: /device:TPU:32 before, /device:TPU:96 now
where the time goes in v3:
time: 63.6 us; the launch traced here: 63.5 us
  Pallas kernels  62.7 us (99%)
  between operations  0.8 us (1%)
    pallas_call x1, Pallas kernels, on_device(): pl.pallas_call(functools.partial(kernel, n_leaf, n_col), out_shape=(jax.S...  53.6 us
    pallas_call x1, Pallas kernels, on_device(): pl.pallas_call(functools.partial(finish, n_leaf, n_col), out_shape=(jax.S...  9.09 us

profile of v3, /device:TPU:96, one launch (start us, length us, event | category | flops | bytes accessed | tf_op | source)
XLA Modules:
  0.0 63.5 jit_solution(727997062860885655)
XLA Ops:
  0.6 53.6 %shard_map.85 = (f32[7,128,128]{2,1,0:T(8,128)}, f32[256,256]{1,0:T(8,128)}) custom-call(f32[2,13,256,256]{3,2,1,0:T(8,128)} %near_h.1, f32[2,256,256]{2,1,0:T(8,128)} %basis_h.1, f32[4,256,256]{2,1,0:T(8,128)} %pb_h.1, s32[2,13]{1,0:T(2,128)} %nbr_h.3, s32[2,13]{1,0:T(2,128)} %live_h.1), custom_call_target="tpu_custom_call" | custom-call | tf_op jit(solution)/shard_map/pallas_call | solution.py:510
  54.3 9.1 %shard_map.86 = (f32[2,64,832]{2,1,0:T(8,128)}, f32[4,64,256]{2,1,0:T(8,128)}, f32[1,64,64]{2,1,0:T(8,128)}) custom-call(f32[7,128,128]{2,1,0:T(8,128)} %get-tuple-element.5.ring_h, f32[256,256]{1,0:T(8,128)} %get-tuple-element.6.joined_h, f32[1,256,256]{2,1,0:T(8,128)} %gb_h.1, s32[2,13]{1,0:T(2,128)} %nbr_h.3), custom_call_target="tpu_custom_call" | custom-call | tf_op jit(solution)/shard_map/pallas_call | solution.py:554

commit v4 on v3

--- a/solution.py
+++ b/solution.py
@@ -280,7 +280,6 @@
             turn(4)
 
     weights = eliminate(diags, [basis_v[0], basis_v[1]], early)
-    relay(1)
 
     v, vt = [], []
     for i in range(2):
@@ -322,6 +321,7 @@
     for e in (2, 4):
         out_and_mine(e)
         sends[e].start()
+    relay(1)
     for e in (1, 5):
         turn(e)
         out_and_mine(e)
@@ -383,39 +383,33 @@
     of = lax.broadcasted_iota(jnp.int32, (SK, 128), 1) // SK + 2 * half
     piece = jnp.where(of == parent, both[SK:], both[:SK])
     share[...] = piece
-    spreads = {}
-    for k in (3, 5, 2, 6, 1, 7):
-        spreads[k] = pltpu.make_async_remote_copy(
+    spreads = []
+    for k in range(1, n_col):
+        spreads.append(
+            pltpu.make_async_remote_copy(
+                src_ref=share,
+                dst_ref=shares.at[col],
+                send_sem=e_send.at[k - 1],
+                recv_sem=e_recv.at[k - 1],
+                device_id=(row, lax.rem(col + k, n_col)),
+                device_id_type=MESH,
+            )
+        )
+    for k in (4, 3, 5, 2, 6, 1, 7):
+        spreads[k - 1].start()
+    shares[col] = piece
+    ring_save = pltpu.make_async_copy(ring.at[4:11], ring_o, save_sem.at[0])
+    ring_save.start()
+
+    for k in range(1, n_col):
+        pltpu.make_async_remote_copy(
             src_ref=share,
-            dst_ref=shares.at[col],
+            dst_ref=shares.at[lax.rem(col - k + n_col, n_col)],
             send_sem=e_send.at[k - 1],
             recv_sem=e_recv.at[k - 1],
             device_id=(row, lax.rem(col + k, n_col)),
             device_id_type=MESH,
-        )
-        spreads[k].start()
-    shares[col] = piece
-    ring_save = pltpu.make_async_copy(ring.at[4:11], ring_o, save_sem.at[0])
-    ring_save.start()
-
-    onwards = []
-    for k, step, side in ((3, 1, 0), (5, n_col - 1, 1)):
-        spreads[k].wait_recv()
-        source = lax.rem(col - k + n_col, n_col)
-        onward = pltpu.make_async_remote_copy(
-            src_ref=shares.at[source, pl.ds(32 * side, 32)],
-            dst_ref=shares.at[source, pl.ds(32 * side, 32)],
-            send_sem=r_sem.at[side],
-            recv_sem=r_sem.at[2 + side],
-            device_id=(row, lax.rem(col + step, n_col)),
-            device_id_type=MESH,
-        )
-        onward.start()
-        onwards.append(onward)
-    for k in (2, 6, 1, 7):
-        spreads[k].wait_recv()
-    for onward in onwards:
-        onward.wait_recv()
+        ).wait_recv()
     rows = [jnp.concatenate([shares[2 * p], shares[2 * p + 1]], axis=1) for p in range(4)]
     summed = jnp.concatenate(rows, axis=0)
     joined[...] = summed + summed.T
@@ -429,10 +423,8 @@
         sends[e].wait_send()
     own_copy.wait_send()
     mixed_copy.wait_send()
-    for k in spreads:
-        spreads[k].wait_send()
-    for onward in onwards:
-        onward.wait_send()
+    for spread in spreads:
+        spread.wait_send()
     ring_save.wait()
     joined_save.wait()
 

time: 63.6 us -> 58.9 us (0.926)
  the two profiles are of different devices: /device:TPU:96 before, /device:TPU:32 now
where the time goes in v4:
time: 58.9 us; the launch traced here: 58.8 us
  Pallas kernels  58 us (98%)
  between operations  0.8 us (1%)
    pallas_call x1, Pallas kernels, on_device(): pl.pallas_call(functools.partial(kernel, n_leaf, n_col), out_shape=(jax.S...  48.9 us
    pallas_call x1, Pallas kernels, on_device(): pl.pallas_call(functools.partial(finish, n_leaf, n_col), out_shape=(jax.S...  9.09 us

profile of v4, /device:TPU:32, one launch (start us, length us, event | category | flops | bytes accessed | tf_op | source)
XLA Modules:
  0.0 58.8 jit_solution(13315046979673851990)
XLA Ops:
  0.6 48.9 %shard_map.85 = (f32[7,128,128]{2,1,0:T(8,128)}, f32[256,256]{1,0:T(8,128)}) custom-call(f32[2,13,256,256]{3,2,1,0:T(8,128)} %near_h.1, f32[2,256,256]{2,1,0:T(8,128)} %basis_h.1, f32[4,256,256]{2,1,0:T(8,128)} %pb_h.1, s32[2,13]{1,0:T(2,128)} %nbr_h.3, s32[2,13]{1,0:T(2,128)} %live_h.1), custom_call_target="tpu_custom_call" | custom-call | tf_op jit(solution)/shard_map/pallas_call | solution.py:502
  49.6 9.1 %shard_map.86 = (f32[2,64,832]{2,1,0:T(8,128)}, f32[4,64,256]{2,1,0:T(8,128)}, f32[1,64,64]{2,1,0:T(8,128)}) custom-call(f32[7,128,128]{2,1,0:T(8,128)} %get-tuple-element.5.ring_h, f32[256,256]{1,0:T(8,128)} %get-tuple-element.6.joined_h, f32[1,256,256]{2,1,0:T(8,128)} %gb_h.1, s32[2,13]{1,0:T(2,128)} %nbr_h.3), custom_call_target="tpu_custom_call" | custom-call | tf_op jit(solution)/shard_map/pallas_call | solution.py:546
